TPU v7x, 512 devices: a whole 4x8x8 slice. The times are simulated.
512 devices in a mesh: box: 64 (over y, x, core), samp: 8 (over z).
Axes of the slice: x: 4, y: 8, z: 8, core: 2. Of those that a mesh axis runs over, the one named last changes fastest.
Arguments:
- currents: bfloat16 [2048, 8, 128], P(('box', 'samp')), may hold values from -6 to 6
- radiation: bfloat16 [2048, 2, 2, 512, 128], P(('box', 'samp')), may hold values from -0.1875 to 0.1875
- near_blocks: bfloat16 [2048, 8, 2, 128, 128], P(('box', 'samp')), may hold values from -0.125 to 0.125
- near_src: int32 [2048, 8], P(('box', 'samp')), may hold values from 0 to 2047, as said below
- leaf_parent: int32 [2048], P('box'), may hold values from 0 to 1023, as said below
- leaf_shift: int32 [2048], P('box'), may hold values from 0 to 7
- shift_table: bfloat16 [8, 2, 8192], P(None, None, 'samp'), may hold values from -4 to 4
- interp_idx: int32 [64, 2], P('samp'), may hold values from 0 to 3, as said below
- interp_val: bfloat16 [64, 2, 128, 128], P('samp'), may hold values from -0.375 to 0.375
- top_src: int32 [1024, 16], P('box'), may hold values from 0 to 1023, as said below
- top_disp: int32 [1024, 16], P('box'), may hold values from 0 to 31
- trans_table: bfloat16 [32, 2, 8192], P(None, None, 'samp'), may hold values from -1 to 1
Outputs:
- matvec: float32 [2048, 8, 128], P(('box', 'samp'))
Inputs may be any that keep to these rules, and one draw needn't show every extreme that they name: `near_src`: entry 0 of a leaf's row is the leaf itself; every entry lies in the 4 leaves of the leaf's own device or of the devices just before and after it in box+samp order (leaves numbered box-major), and these ends are reached. `leaf_parent`: the parent of leaf l lies in its box group: its value divided by 16 equals l divided by 32. `interp_idx`: the 2 entries of a row differ. `top_src`: a source of top box t is another box of t's group (t // 16), or one of the last 8 boxes of the group before it, or one of the first 8 boxes of the group after it; both rims are reached.
All inputs are finite; a program needn't handle non-finite values.
Results may differ from a plain program's by a relative error of at most 0.013.
Values may be sent and summed in bfloat16 or wider, within the bound.
A program may use at most 64 MiB of HBM per device.

v0:
```python
import jax
import jax.numpy as jnp
from jax import lax
from jax.sharding import PartitionSpec as P

HIGHEST = lax.Precision.HIGHEST


def with_halo(cells, sides, width):
    for axis, dim in sides:
        count = lax.axis_size(axis)
        ends = count - 1
        head = lax.slice_in_dim(cells, 0, width, axis=dim)
        tail = lax.slice_in_dim(cells, cells.shape[dim] - width, cells.shape[dim], axis=dim)
        cells = jnp.concatenate(
            [
                lax.ppermute(tail, axis, [(i, (i + 1) % count) for i in range(ends)]),
                cells,
                lax.ppermute(head, axis, [((i + 1) % count, i) for i in range(ends)]),
            ],
            axis=dim,
        )
    return cells


def complex_mul(a_real, a_imag, b_real, b_imag):
    return (a_real * b_real - a_imag * b_imag, a_real * b_imag + a_imag * b_real)


def contract(form, first_op, second_op):
    return jnp.einsum(form, first_op, second_op, preferred_element_type=jnp.float32)


def per_device(
    currents,
    radiation,
    near_blocks,
    near_src,
    leaf_parent,
    leaf_shift,
    shift_table,
    interp_idx,
    interp_val,
    top_src,
    top_disp,
    trans_table,
):
    leaf_count = currents.shape[0]
    half_comp = currents.shape[1]
    excite = half_comp // 2
    comps = 2 * half_comp
    samp_count = lax.axis_size("samp")
    group_index = lax.axis_index("box")
    first_leaf = (group_index * samp_count + lax.axis_index("samp")) * leaf_count
    top_count = top_src.shape[0]
    block_size = interp_val.shape[2]
    leaf_samples = radiation.shape[3]
    in_blocks = leaf_samples // block_size
    local_blocks = interp_val.shape[0]
    local_samples = local_blocks * block_size
    neighbours = with_halo(currents, ((("box", "samp"), 0),), leaf_count)
    rad_real = radiation[:, :, 0]
    rad_imag = radiation[:, :, 1]
    form_out = "lpqu,leu->lpeq"
    out_real = contract(form_out, rad_real, currents[:, :excite]) - contract(
        form_out, rad_imag, currents[:, excite:]
    )
    out_imag = contract(form_out, rad_real, currents[:, excite:]) + contract(
        form_out, rad_imag, currents[:, :excite]
    )
    patterns = jnp.concatenate(
        [
            out_real.reshape(leaf_count, half_comp, leaf_samples),
            out_imag.reshape(leaf_count, half_comp, leaf_samples),
        ],
        axis=1,
    ).astype(jnp.bfloat16)
    piece = lax.all_gather(patterns, "samp", axis=0, tiled=True)
    piece_rows = piece.shape[0]
    picked = piece.reshape(piece_rows, comps, in_blocks, block_size)[:, :, interp_idx, :]
    moved_rows = contract("lcbri,brki->lcbk", picked, interp_val)
    moved = moved_rows.reshape(piece_rows, comps, local_samples)
    shift_onehot = (leaf_shift[:, None] == jnp.arange(shift_table.shape[0])[None, :]).astype(
        jnp.bfloat16
    )
    shift_rows = contract("ln,nrk->lrk", shift_onehot, shift_table)
    shift_real = shift_rows[:, 0:1]
    shift_imag = shift_rows[:, 1:2]
    up_real, up_imag = complex_mul(
        moved[:, :half_comp], moved[:, half_comp:], shift_real, shift_imag
    )
    shifted = jnp.concatenate([up_real, up_imag], axis=1)
    parent_local = leaf_parent - group_index * top_count
    member = parent_local[None, :] == jnp.arange(top_count)[:, None]
    top_patterns = jnp.einsum(
        "tl,lck->tck", member.astype(jnp.float32), shifted, precision=HIGHEST
    ).astype(jnp.bfloat16)
    padded = with_halo(top_patterns, (("box", 0),), top_count)
    base_index = group_index * top_count - top_count
    disp_count = trans_table.shape[0]

    def add_entry(entry, total):
        source_rows = jnp.take(padded, top_src[:, entry] - base_index, axis=0).astype(jnp.float32)
        disp_onehot = (top_disp[:, entry][:, None] == jnp.arange(disp_count)[None, :]).astype(
            jnp.bfloat16
        )
        coeff = contract("tn,nrk->trk", disp_onehot, trans_table)
        part_real, part_imag = complex_mul(
            coeff[:, 0:1], coeff[:, 1:2], source_rows[:, :half_comp], source_rows[:, half_comp:]
        )
        return total + jnp.concatenate([part_real, part_imag], axis=1)

    incoming = lax.fori_loop(
        0, top_src.shape[1], add_entry, jnp.zeros((top_count, comps, local_samples), jnp.float32)
    ).astype(jnp.bfloat16)
    spread = contract("tl,tck->lck", member.astype(jnp.bfloat16), incoming)
    down_real, down_imag = complex_mul(
        shift_real, -shift_imag, spread[:, :half_comp], spread[:, half_comp:]
    )
    down = jnp.concatenate([down_real, down_imag], axis=1).astype(jnp.bfloat16)
    block_onehot = (interp_idx[:, :, None] == jnp.arange(in_blocks)[None, None, :]).astype(
        jnp.float32
    )
    parts = contract(
        "lcbk,brki->lcbri",
        down.reshape(leaf_count * lax.axis_size("samp"), comps, local_blocks, block_size),
        interp_val,
    )
    folded = jnp.einsum("lcbri,brq->lcqi", parts, block_onehot, precision=HIGHEST)
    far = lax.psum_scatter(
        folded.reshape(leaf_count * lax.axis_size("samp"), comps, leaf_samples).astype(
            jnp.bfloat16
        ),
        "samp",
        scatter_dimension=0,
        tiled=True,
    )
    far_real = far[:, :half_comp].reshape(leaf_count, 2, excite, leaf_samples)
    far_imag = far[:, half_comp:].reshape(leaf_count, 2, excite, leaf_samples)
    form_back = "lpqu,lpeq->leu"
    recv_real = contract(form_back, rad_real, far_real) + contract(form_back, rad_imag, far_imag)
    recv_imag = contract(form_back, rad_real, far_imag) - contract(form_back, rad_imag, far_real)
    near_rows = jnp.take(neighbours, near_src - first_leaf + leaf_count, axis=0)
    block_real = near_blocks[:, :, 0]
    block_imag = near_blocks[:, :, 1]
    form_near = "lnuv,lnev->leu"
    near_real = contract(form_near, block_real, near_rows[:, :, :excite]) - contract(
        form_near, block_imag, near_rows[:, :, excite:]
    )
    near_imag = contract(form_near, block_real, near_rows[:, :, excite:]) + contract(
        form_near, block_imag, near_rows[:, :, :excite]
    )
    return jnp.concatenate([recv_real + near_real, recv_imag + near_imag], axis=1)


def solution(mesh):
    placed = (
        P(("box", "samp"), None, None),
        P(("box", "samp"), None, None, None, None),
        P(("box", "samp"), None, None, None, None),
        P(("box", "samp"), None),
        P("box"),
        P("box"),
        P(None, None, "samp"),
        P("samp", None),
        P("samp", None, None, None),
        P("box", None),
        P("box", None),
        P(None, None, "samp"),
    )
    return jax.shard_map(
        per_device,
        mesh=mesh,
        in_specs=placed,
        out_specs=P(("box", "samp"), None, None),
        check_vma=False,
    )
```

profile of v0, /device:TPU:4, one launch (start us, length us, event | category | flops | bytes accessed | tf_op | source)
XLA Modules:
  0.0 176.0 jit_solution(13195029039709390717)
XLA Ops:
  6.6 1.8 %fusion.46 = f32[4,4,2,512]{3,1,2,0:T(4,128)S(1)} fusion(bf16[4,2,2,512,128]{4,3,2,1,0:T(8,128)(2,1)} %param.15, bf16[4,8,128]{2,1,0:T(8,128)(2,1)} %param.14), kind=kOutput, calls=%fused_computation.65 | convolution fusion | flops 4194304 | bytes 1118208 | tf_op jit(solution)/shard_map/lpqu,leu->lpeq/dot_general | solution.py:31
  8.4 1.6 fusion.44
  10.3 0.4 fusion.25
  10.7 0.4 fusion.24
  11.1 31.6 %all_gather.3 = bf16[32,16,512]{2,1,0:T(8,128)(2,1)S(1)} all-gather(bf16[4,16,512]{2,1,0:T(8,128)(2,1)S(1)} %pad_maximum_fusion.1), channel_id=1, replica_groups=mesh['box'=64,'samp'=8] {'samp'}, dimensions={0}, use_global_device_ids=true | all-gather | bytes 589824 | tf_op jit(solution)/shard_map/all_gather | solution.py:78
  43.1 1.1 gather_fusion.1
  44.2 0.7 convolution_bitcast_fusion.1
  44.9 2.5 %copy.92 = f32[32,16,8,128]{3,2,0,1:T(8,128)} copy(f32[32,16,8,128]{3,1,0,2:T(8,128)S(1)} %convolution_bitcast_fusion.1) | data formatting | bytes 4194304 | tf_op jit(solution)/shard_map/reshape | solution.py:82
  47.4 1.7 reshape.96
  49.5 0.8 fusion.16
  50.4 1.9 %collective-permute-start = (bf16[16,16,1024]{2,0,1:T(8,128)(2,1)S(1)}, bf16[16,16,1024]{2,0,1:T(8,128)(2,1)S(1)}, u32[]{:S(2)}, u32[]{:S(2)}) collective-permute-start(bf16[16,16,1024]{2,0,1:T(8,128)(2,1)S(1)} %fusion.16), channel_id=1, source_target_pairs={{0,8},{8,16},{16,24},{24,32},{32,40},{40,48},{48,56},{56,64},{64,7... | collective-permute-start | bytes 1572872 | tf_op jit(solution)/shard_map/ppermute | solution.py:17
  52.3 3.8 %collective-permute-start.1 = (bf16[16,16,1024]{2,0,1:T(8,128)(2,1)S(1)}, bf16[16,16,1024]{2,0,1:T(8,128)(2,1)}, u32[]{:S(2)}, u32[]{:S(2)}) collective-permute-start(bf16[16,16,1024]{2,0,1:T(8,128)(2,1)S(1)} %fusion.16), channel_id=1, source_target_pairs={{8,0},{16,8},{24,16},{32,24},{40,32},{48,40},{56,48},{64,56},{72,6... | collective-permute-start | bytes 1572872 | tf_op jit(solution)/shard_map/ppermute | solution.py:19
  56.3 4.5 %collective-permute-done = bf16[16,16,1024]{2,0,1:T(8,128)(2,1)S(1)} collective-permute-done((bf16[16,16,1024]{2,0,1:T(8,128)(2,1)S(1)}, bf16[16,16,1024]{2,0,1:T(8,128)(2,1)S(1)}, u32[]{:S(2)}, u32[]{:S(2)}) %collective-permute-start) | collective-permute-done | bytes 524320 | tf_op jit(solution)/shard_map/ppermute | solution.py:17
  60.9 1.8 collective-permute-done.1
  62.6 1.2 pad_maximum_fusion
  63.8 2.0 %copy.70 = bf16[48,16,1024]{2,1,0:T(8,128)(2,1)} copy(bf16[48,16,1024]{2,0,1:T(8,128)(2,1)S(1)} %pad_maximum_fusion) | data formatting | bytes 3145728
  65.9 48.1 %while.14 = (s32[]{:T(128)}, f32[16,16,1024]{2,1,0:T(8,128)S(1)}, s32[16,16]{0,1:T(8,128)S(1)}, bf16[32,2,1024]{2,0,1:T(8,128)(2,1)S(1)}, s32[16,16]{0,1:T(8,128...) while((s32[]{:T(128)}, f32[16,16,1024]{2,1,0:T(8,128)S(1)}, ...), condition=%wide.region_1.0_spmd.clone, body=%wide.region_0.1_spmd.clone.sunk | while | flops 4195955 | bytes 8524371 | solution.py:113
  65.9 2.0 %gather_fusion = bf16[16,16,1024]{2,1,0:T(8,128)(2,1)S(1)} fusion(bf16[48,16,1024]{2,1,0:T(8,128)(2,1)} %get-tuple-element.292, s32[1024]{0:T(1024)S(1)} %pad_clamp_fusion.4), kind=kCustom, calls=%fused_computation.clone.clone.1 | custom fusion | bytes 1048640 | tf_op jit(solution)/shard_map/while/body/eval_jaxpr/jit(_take)/gather | solution.py:103
  68.5 0.3 maximum_add_fusion.2
  68.9 2.0 %gather_fusion = bf16[16,16,1024]{2,1,0:T(8,128)(2,1)S(1)} fusion(bf16[48,16,1024]{2,1,0:T(8,128)(2,1)} %get-tuple-element.292, s32[1024]{0:T(1024)S(1)} %pad_clamp_fusion.4), kind=kCustom, calls=%fused_computation.clone.clone.1 | custom fusion | bytes 1048640 | tf_op jit(solution)/shard_map/while/body/eval_jaxpr/jit(_take)/gather | solution.py:103
  71.5 0.3 maximum_add_fusion.2
  71.9 2.0 %gather_fusion = bf16[16,16,1024]{2,1,0:T(8,128)(2,1)S(1)} fusion(bf16[48,16,1024]{2,1,0:T(8,128)(2,1)} %get-tuple-element.292, s32[1024]{0:T(1024)S(1)} %pad_clamp_fusion.4), kind=kCustom, calls=%fused_computation.clone.clone.1 | custom fusion | bytes 1048640 | tf_op jit(solution)/shard_map/while/body/eval_jaxpr/jit(_take)/gather | solution.py:103
  74.5 0.3 maximum_add_fusion.2
  74.9 2.0 %gather_fusion = bf16[16,16,1024]{2,1,0:T(8,128)(2,1)S(1)} fusion(bf16[48,16,1024]{2,1,0:T(8,128)(2,1)} %get-tuple-element.292, s32[1024]{0:T(1024)S(1)} %pad_clamp_fusion.4), kind=kCustom, calls=%fused_computation.clone.clone.1 | custom fusion | bytes 1048640 | tf_op jit(solution)/shard_map/while/body/eval_jaxpr/jit(_take)/gather | solution.py:103
  77.5 0.3 maximum_add_fusion.2
  77.9 2.0 %gather_fusion = bf16[16,16,1024]{2,1,0:T(8,128)(2,1)S(1)} fusion(bf16[48,16,1024]{2,1,0:T(8,128)(2,1)} %get-tuple-element.292, s32[1024]{0:T(1024)S(1)} %pad_clamp_fusion.4), kind=kCustom, calls=%fused_computation.clone.clone.1 | custom fusion | bytes 1048640 | tf_op jit(solution)/shard_map/while/body/eval_jaxpr/jit(_take)/gather | solution.py:103
  80.5 0.3 maximum_add_fusion.2
  80.9 2.0 %gather_fusion = bf16[16,16,1024]{2,1,0:T(8,128)(2,1)S(1)} fusion(bf16[48,16,1024]{2,1,0:T(8,128)(2,1)} %get-tuple-element.292, s32[1024]{0:T(1024)S(1)} %pad_clamp_fusion.4), kind=kCustom, calls=%fused_computation.clone.clone.1 | custom fusion | bytes 1048640 | tf_op jit(solution)/shard_map/while/body/eval_jaxpr/jit(_take)/gather | solution.py:103
  83.5 0.3 maximum_add_fusion.2
  83.9 2.0 %gather_fusion = bf16[16,16,1024]{2,1,0:T(8,128)(2,1)S(1)} fusion(bf16[48,16,1024]{2,1,0:T(8,128)(2,1)} %get-tuple-element.292, s32[1024]{0:T(1024)S(1)} %pad_clamp_fusion.4), kind=kCustom, calls=%fused_computation.clone.clone.1 | custom fusion | bytes 1048640 | tf_op jit(solution)/shard_map/while/body/eval_jaxpr/jit(_take)/gather | solution.py:103
  86.5 0.3 maximum_add_fusion.2
  86.9 2.0 %gather_fusion = bf16[16,16,1024]{2,1,0:T(8,128)(2,1)S(1)} fusion(bf16[48,16,1024]{2,1,0:T(8,128)(2,1)} %get-tuple-element.292, s32[1024]{0:T(1024)S(1)} %pad_clamp_fusion.4), kind=kCustom, calls=%fused_computation.clone.clone.1 | custom fusion | bytes 1048640 | tf_op jit(solution)/shard_map/while/body/eval_jaxpr/jit(_take)/gather | solution.py:103
  89.5 0.3 maximum_add_fusion.2
  90.0 2.0 %gather_fusion = bf16[16,16,1024]{2,1,0:T(8,128)(2,1)S(1)} fusion(bf16[48,16,1024]{2,1,0:T(8,128)(2,1)} %get-tuple-element.292, s32[1024]{0:T(1024)S(1)} %pad_clamp_fusion.4), kind=kCustom, calls=%fused_computation.clone.clone.1 | custom fusion | bytes 1048640 | tf_op jit(solution)/shard_map/while/body/eval_jaxpr/jit(_take)/gather | solution.py:103
  92.6 0.3 maximum_add_fusion.2
  93.0 2.0 %gather_fusion = bf16[16,16,1024]{2,1,0:T(8,128)(2,1)S(1)} fusion(bf16[48,16,1024]{2,1,0:T(8,128)(2,1)} %get-tuple-element.292, s32[1024]{0:T(1024)S(1)} %pad_clamp_fusion.4), kind=kCustom, calls=%fused_computation.clone.clone.1 | custom fusion | bytes 1048640 | tf_op jit(solution)/shard_map/while/body/eval_jaxpr/jit(_take)/gather | solution.py:103
  95.6 0.3 maximum_add_fusion.2
  96.0 2.0 %gather_fusion = bf16[16,16,1024]{2,1,0:T(8,128)(2,1)S(1)} fusion(bf16[48,16,1024]{2,1,0:T(8,128)(2,1)} %get-tuple-element.292, s32[1024]{0:T(1024)S(1)} %pad_clamp_fusion.4), kind=kCustom, calls=%fused_computation.clone.clone.1 | custom fusion | bytes 1048640 | tf_op jit(solution)/shard_map/while/body/eval_jaxpr/jit(_take)/gather | solution.py:103
  98.6 0.3 maximum_add_fusion.2
  99.0 2.0 %gather_fusion = bf16[16,16,1024]{2,1,0:T(8,128)(2,1)S(1)} fusion(bf16[48,16,1024]{2,1,0:T(8,128)(2,1)} %get-tuple-element.292, s32[1024]{0:T(1024)S(1)} %pad_clamp_fusion.4), kind=kCustom, calls=%fused_computation.clone.clone.1 | custom fusion | bytes 1048640 | tf_op jit(solution)/shard_map/while/body/eval_jaxpr/jit(_take)/gather | solution.py:103
  101.6 0.3 maximum_add_fusion.2
  102.0 2.0 %gather_fusion = bf16[16,16,1024]{2,1,0:T(8,128)(2,1)S(1)} fusion(bf16[48,16,1024]{2,1,0:T(8,128)(2,1)} %get-tuple-element.292, s32[1024]{0:T(1024)S(1)} %pad_clamp_fusion.4), kind=kCustom, calls=%fused_computation.clone.clone.1 | custom fusion | bytes 1048640 | tf_op jit(solution)/shard_map/while/body/eval_jaxpr/jit(_take)/gather | solution.py:103
  105.0 2.0 %gather_fusion = bf16[16,16,1024]{2,1,0:T(8,128)(2,1)S(1)} fusion(bf16[48,16,1024]{2,1,0:T(8,128)(2,1)} %get-tuple-element.292, s32[1024]{0:T(1024)S(1)} %pad_clamp_fusion.4), kind=kCustom, calls=%fused_computation.clone.clone.1 | custom fusion | bytes 1048640 | tf_op jit(solution)/shard_map/while/body/eval_jaxpr/jit(_take)/gather | solution.py:103
  107.6 0.3 maximum_add_fusion.2
  108.0 2.0 %gather_fusion = bf16[16,16,1024]{2,1,0:T(8,128)(2,1)S(1)} fusion(bf16[48,16,1024]{2,1,0:T(8,128)(2,1)} %get-tuple-element.292, s32[1024]{0:T(1024)S(1)} %pad_clamp_fusion.4), kind=kCustom, calls=%fused_computation.clone.clone.1 | custom fusion | bytes 1048640 | tf_op jit(solution)/shard_map/while/body/eval_jaxpr/jit(_take)/gather | solution.py:103
  110.6 0.3 maximum_add_fusion.2
  111.0 2.0 %gather_fusion = bf16[16,16,1024]{2,1,0:T(8,128)(2,1)S(1)} fusion(bf16[48,16,1024]{2,1,0:T(8,128)(2,1)} %get-tuple-element.292, s32[1024]{0:T(1024)S(1)} %pad_clamp_fusion.4), kind=kCustom, calls=%fused_computation.clone.clone.1 | custom fusion | bytes 1048640 | tf_op jit(solution)/shard_map/while/body/eval_jaxpr/jit(_take)/gather | solution.py:103
  113.6 0.3 maximum_add_fusion.2
  114.0 0.5 fusion.62
  115.8 0.7 convolution_bitcast_fusion
  116.5 4.0 %fusion.19 = bf16[32,16,4,128]{3,2,1,0:T(4,128)(2,1)S(1)} fusion(f32[32,16,8,2,128]{4,1,3,0,2:T(8,128)S(1)} %convolution_bitcast_fusion, s32[8,2]{0,1:T(2,128)S(1)} %copy-done.9), kind=kOutput, calls=%fused_computation.29 | convolution fusion | flops 50593856 | bytes 4718656 | tf_op jit(solution)/shard_map/lcbri,brq->lcqi/dot_general | solution.py:129
  120.6 1.0 convert_element_type.36
  121.6 3.7 %collective-permute-start.2 = (bf16[4,8,128]{2,1,0:T(8,128)(2,1)S(1)}, bf16[4,8,128]{2,1,0:T(8,128)(2,1)S(1)}, u32[]{:S(2)}, u32[]{:S(2)}) collective-permute-start(bf16[4,8,128]{2,1,0:T(8,128)(2,1)S(1)} %copy-done.4), channel_id=1, source_target_pairs={{0,1},{1,2},{2,3},{3,4},{4,5},{5,6},{6,7},{7,8},{8,9},{9,10},{10,1... | collective-permute-start | bytes 24584 | tf_op jit(solution)/shard_map/ppermute | solution.py:17
  125.3 4.6 %collective-permute-start.3 = (bf16[4,8,128]{2,1,0:T(8,128)(2,1)S(1)}, bf16[4,8,128]{2,1,0:T(8,128)(2,1)S(1)}, u32[]{:S(2)}, u32[]{:S(2)}) collective-permute-start(bf16[4,8,128]{2,1,0:T(8,128)(2,1)S(1)} %copy-done.4), channel_id=1, source_target_pairs={{1,0},{2,1},{3,2},{4,3},{5,4},{6,5},{7,6},{8,7},{9,8},{10,9},{11,1... | collective-permute-start | bytes 24584 | tf_op jit(solution)/shard_map/ppermute | solution.py:19
  130.0 1.2 collective-permute-done.3
  131.2 0.6 gather_fusion.2
  131.9 1.6 convolution_bitcast_fusion.7
  133.5 1.6 convolution_bitcast_fusion.3
  135.2 29.9 %reduce-scatter.2.cloned.1.call-done = bf16[4,16,512]{2,1,0:T(8,128)(2,1)} async-done(((bf16[32,16,512]{2,1,0:T(8,128)(2,1)}), bf16[4,16,512]{2,1,0:T(8,128)(2,1)}) %reduce-scatter.2.cloned.1.call-update) | async-done | bytes 65552 | tf_op jit(solution)/shard_map/reduce_scatter | solution.py:130
  165.0 0.8 fusion.91
  166.9 0.8 copy-done.3
  167.7 0.4 fusion.30
  168.1 0.4 fusion.27
  168.5 0.6 pad_maximum_fusion.3
  (174 shorter events, 13.6 us)
Async XLA Ops:
  6.5 37.6 %copy-start = (bf16[8,2,128,128]{3,2,1,0:T(8,128)(2,1)S(1)}, bf16[8,2,128,128]{3,2,1,0:T(8,128)(2,1)}, u32[]{:S(2)}) copy-start(bf16[8,2,128,128]{3,2,1,0:T(8,128)(2,1)} %param.22) | copy-start | bytes 1572868
  6.5 3.7 %copy-start.4 = (bf16[4,8,128]{2,1,0:T(8,128)(2,1)S(1)}, bf16[4,8,128]{2,1,0:T(8,128)(2,1)}, u32[]{:S(2)}) copy-start(bf16[4,8,128]{2,1,0:T(8,128)(2,1)} %param.14) | copy-start | bytes 24580
  6.5 3.7 %copy-start.1 = (bf16[4,2,2,512,128]{4,3,2,1,0:T(8,128)(2,1)S(1)}, bf16[4,2,2,512,128]{4,3,2,1,0:T(8,128)(2,1)}, u32[]{:S(2)}) copy-start(bf16[4,2,2,512,128]{4,3,2,1,0:T(8,128)(2,1)} %param.15) | copy-start | bytes 6291460
  6.5 3.4 %copy-start.11 = (s32[32]{0:T(128)S(1)}, s32[32]{0:T(128)}, u32[]{:S(2)}) copy-start(s32[32]{0:T(128)} %param.19) | copy-start | bytes 388
  6.5 3.4 %copy-start.6 = (bf16[8,2,1024]{2,1,0:T(2,128)(2,1)S(1)}, bf16[8,2,1024]{2,1,0:T(2,128)(2,1)}, u32[]{:S(2)}) copy-start(bf16[8,2,1024]{2,1,0:T(2,128)(2,1)} %param.20) | copy-start | bytes 98308
  6.5 158.5 %reduce-scatter.2.cloned.1.call-start = ((), (), s32[]{:S(2)}) async-start(), calls=%async_computation.1 | async-start | bytes 589824 | tf_op jit(solution)/shard_map/reduce_scatter | solution.py:130
  10.3 32.6 %copy-start.9 = (s32[8,2]{0,1:T(2,128)S(1)}, s32[8,2]{0,1:T(2,128)}, u32[]{:S(2)}) copy-start(s32[8,2]{0,1:T(2,128)} %param.21) | copy-start | bytes 196
  47.4 1.7 copy-start.12
  49.5 6.7 %copy-start.5 = (bf16[32,2,1024]{2,1,0:T(2,128)(2,1)S(1)}, bf16[32,2,1024]{2,1,0:T(2,128)(2,1)}, u32[]{:S(2)}) copy-start(bf16[32,2,1024]{2,1,0:T(2,128)(2,1)} %param.25) | copy-start | bytes 393220
  49.5 6.7 %copy-start.7 = (s32[16,16]{1,0:T(8,128)S(1)}, s32[16,16]{1,0:T(8,128)}, u32[]{:S(2)}) copy-start(s32[16,16]{1,0:T(8,128)} %param.24) | copy-start | bytes 3076
  49.5 6.8 %copy-start.8 = (s32[16,16]{1,0:T(8,128)S(1)}, s32[16,16]{1,0:T(8,128)}, u32[]{:S(2)}) copy-start(s32[16,16]{1,0:T(8,128)} %param.23) | copy-start | bytes 3076
  50.4 10.5 %collective-permute-start = (bf16[16,16,1024]{2,0,1:T(8,128)(2,1)S(1)}, bf16[16,16,1024]{2,0,1:T(8,128)(2,1)S(1)}, u32[]{:S(2)}, u32[]{:S(2)}) collective-permute-start(bf16[16,16,1024]{2,0,1:T(8,128)(2,1)S(1)} %fusion.16), channel_id=1, source_target_pairs={{0,8},{8,16},{16,24},{24,32},{32,40},{40,48},{48,56},{56,64},{64,7... | collective-permute-start | bytes 1572872 | tf_op jit(solution)/shard_map/ppermute | solution.py:17
  52.3 10.3 %collective-permute-start.1 = (bf16[16,16,1024]{2,0,1:T(8,128)(2,1)S(1)}, bf16[16,16,1024]{2,0,1:T(8,128)(2,1)}, u32[]{:S(2)}, u32[]{:S(2)}) collective-permute-start(bf16[16,16,1024]{2,0,1:T(8,128)(2,1)S(1)} %fusion.16), channel_id=1, source_target_pairs={{8,0},{16,8},{24,16},{32,24},{40,32},{48,40},{56,48},{64,56},{72,6... | collective-permute-start | bytes 1572872 | tf_op jit(solution)/shard_map/ppermute | solution.py:19
  116.5 13.4 %copy-start.10 = (s32[4,8]{1,0:T(4,128)S(1)}, s32[4,8]{1,0:T(4,128)}, u32[]{:S(2)}) copy-start(s32[4,8]{1,0:T(4,128)} %param.17) | copy-start | bytes 388
  120.6 45.3 %copy-start.2 = (bf16[4,2,2,512,128]{4,3,2,1,0:T(8,128)(2,1)S(1)}, bf16[4,2,2,512,128]{4,3,2,1,0:T(8,128)(2,1)}, u32[]{:S(2)}) copy-start(bf16[4,2,2,512,128]{4,3,2,1,0:T(8,128)(2,1)} %param.15) | copy-start | bytes 6291460
  121.6 8.4 %collective-permute-start.2 = (bf16[4,8,128]{2,1,0:T(8,128)(2,1)S(1)}, bf16[4,8,128]{2,1,0:T(8,128)(2,1)S(1)}, u32[]{:S(2)}, u32[]{:S(2)}) collective-permute-start(bf16[4,8,128]{2,1,0:T(8,128)(2,1)S(1)} %copy-done.4), channel_id=1, source_target_pairs={{0,1},{1,2},{2,3},{3,4},{4,5},{5,6},{6,7},{7,8},{8,9},{9,10},{10,1... | collective-permute-start | bytes 24584 | tf_op jit(solution)/shard_map/ppermute | solution.py:17
  125.3 5.9 %collective-permute-start.3 = (bf16[4,8,128]{2,1,0:T(8,128)(2,1)S(1)}, bf16[4,8,128]{2,1,0:T(8,128)(2,1)S(1)}, u32[]{:S(2)}, u32[]{:S(2)}) collective-permute-start(bf16[4,8,128]{2,1,0:T(8,128)(2,1)S(1)} %copy-done.4), channel_id=1, source_target_pairs={{1,0},{2,1},{3,2},{4,3},{5,4},{6,5},{7,6},{8,7},{9,8},{10,9},{11,1... | collective-permute-start | bytes 24584 | tf_op jit(solution)/shard_map/ppermute | solution.py:19
  166.1 1.6 copy-start.3
Sparse Core Ops, SparseCore 0:
  121.7 43.2 reduce-scatter.1
where the time goes:
time: 177 us; the launch traced here: 176 us
  local copies, waits for them, and re-layouts  44.3 us (25%)
  waiting for transfers between devices  37.4 us (21%)
  blocking collectives  31.6 us (18%)
  matrix products  19.5 us (11%)
  other arithmetic  14.1 us (8%)
  starting transfers between devices  14 us (8%)
  between operations  13.8 us (8%)
    gather x16, local copies, waits for them, and re-layouts, add_entry(): jnp.take(padded, top_src[:, entry] - base_index, axis=0).astype(jnp.float32)  31.8 us
    all_gather x1, blocking collectives, per_device(): piece = lax.all_gather(patterns, 'samp', axis=0, tiled=True)  31.6 us
    reduce_scatter x1, waiting for transfers between devices, per_device(): lax.psum_scatter(folded.reshape(leaf_count * lax.axis_size('samp'), comps...  29.9 us
    dot_general x32, matrix products, contract(): jnp.einsum(form, first_op, second_op, preferred_element_type=jnp.float32)  14.6 us
    ppermute x2, starting transfers between devices, with_halo(): lax.ppermute(head, axis, [((i + 1) % count, i) for i in range(ends)])  8.41 us
    ppermute x2, starting transfers between devices, with_halo(): lax.ppermute(tail, axis, [(i, (i + 1) % count) for i in range(ends)])  5.6 us
    add x16, other arithmetic, add_entry(): return total + jnp.concatenate([part_real, part_imag], axis=1)  5.52 us
    ppermute x2, waiting for transfers between devices, with_halo(): lax.ppermute(tail, axis, [(i, (i + 1) % count) for i in range(ends)])  4.53 us
  transfers between devices with their start and end apart: 5, of which 4 were waited for; matrix products, arithmetic and copies ran while one was open for 2% of the time, Pallas kernels for 0%

commit v1 on v0

v1 whole, which is shorter than its diff:
```python
import functools

import jax
import jax.numpy as jnp
from jax import lax
from jax.experimental import pallas as pl
from jax.experimental.pallas import tpu as pltpu
from jax.sharding import PartitionSpec as P

MESH = pl.DeviceIdType.MESH
F32 = jnp.float32
BF16 = jnp.bfloat16
EXC = 4
COMPS = 16
HALF = 8
KL = 512
KD = 1024
BLK = 128
CH = 4
KC = KD // CH
LEAF = 4
SAMP = 8
GL = LEAF * SAMP
TOP = 16
RIM = 8
NEAR = 8
ILIST = 16
NDISP = 32
NSHIFT = 8

O_ORDER = 0
O_CONT = 32
O_LAST = 64
O_HAS = 80
O_SHIFT = 96
O_PARENT = 128
O_NEAR = 160
O_INTERP = 192
O_SRC = 208
O_DISP = 464
N_INTS = 720

NT_DIMS = (((1,), (1,)), ((), ()))
NN_DIMS = (((1,), (0,)), ((), ()))


def dot(a, b, dims):
    return lax.dot_general(a, b, dims, preferred_element_type=F32)


def kernel(
    boxes,
    ints,
    cur_hbm,
    rad_hbm,
    near_hbm,
    shift_hbm,
    val_hbm,
    trans_hbm,
    out_ref,
    nbr,
    xbuf,
    rad,
    near,
    shift_raw,
    val,
    trans_raw,
    w,
    sh,
    tr,
    own,
    ag_r,
    ag_l,
    ag_f,
    shifted,
    seg,
    topbf,
    halo_l,
    halo_r,
    srcf,
    inc,
    down,
    part,
    rs_r,
    rs_l,
    st_r,
    st_l,
    nearacc,
    local_sem,
    cur_sem,
    ag_send,
    ag_recv,
    halo_send,
    halo_recv,
    rs_send,
    rs_recv,
):
    box = lax.axis_index("box")
    samp = lax.axis_index("samp")
    total = boxes * SAMP
    right = (box, lax.rem(samp + 1, SAMP))
    left = (box, lax.rem(samp + SAMP - 1, SAMP))
    box_next = (lax.rem(box + 1, boxes), samp)
    box_prev = (lax.rem(box + boxes - 1, boxes), samp)
    flat = box * SAMP + samp
    flat_up = lax.rem(flat + 1, total)
    flat_dn = lax.rem(flat + total - 1, total)
    dev_up = (flat_up // SAMP, lax.rem(flat_up, SAMP))
    dev_dn = (flat_dn // SAMP, lax.rem(flat_dn, SAMP))

    barrier = pltpu.get_barrier_semaphore()
    for dev in (right, left, box_next, box_prev, dev_up, dev_dn):
        pl.semaphore_signal(barrier, inc=1, device_id=dev, device_id_type=MESH)

    def local(src, dst, index):
        return pltpu.make_async_copy(src, dst, local_sem.at[index])

    cur_copy = local(cur_hbm, nbr.at[pl.ds(LEAF, LEAF)], 0)
    rad_copies = [local(rad_hbm.at[i], rad.at[i], 1 + i) for i in range(LEAF)]
    val_copy = local(val_hbm, val, 5)
    shift_copy = local(shift_hbm, shift_raw, 6)
    trans_copy = local(trans_hbm, trans_raw, 7)
    near_copies = [local(near_hbm.at[i], near.at[i], 8 + i) for i in range(LEAF)]
    cur_copy.start()
    for copy in rad_copies:
        copy.start()
    val_copy.start()
    shift_copy.start()
    trans_copy.start()
    for copy in near_copies:
        copy.start()

    def remote(src, dst, send, recv, dev):
        return pltpu.make_async_remote_copy(
            src_ref=src,
            dst_ref=dst,
            send_sem=send,
            recv_sem=recv,
            device_id=dev,
            device_id_type=MESH,
        )

    def gather_copy(way, step, i):
        buf = ag_r if way == 0 else ag_l
        if step == 0:
            src = own.at[i]
        else:
            src = buf.at[step - 1, i]
        dst = ag_f.at[i] if step == 3 else buf.at[step, i]
        return remote(
            src, dst, ag_send.at[way, step, i], ag_recv.at[way, step, i], (right, left)[way]
        )

    def gather_has(way, step, i):
        return step < 3 or (i < 2) == (way == 0)

    gathers = {
        (way, step, i): gather_copy(way, step, i)
        for step in range(4)
        for i in range(LEAF)
        for way in range(2)
        if gather_has(way, step, i)
    }

    cur_copy.wait()
    for i in range(LEAF):
        x = nbr[LEAF + i].astype(F32)
        c_re, c_im = x[:EXC], x[EXC:]
        zero = jnp.zeros_like(c_re)
        lhs = jnp.concatenate(
            [
                jnp.concatenate([c_re, zero, c_im, zero], axis=0),
                jnp.concatenate([-c_im, zero, c_re, zero], axis=0),
                jnp.concatenate([zero, c_re, zero, c_im], axis=0),
                jnp.concatenate([zero, -c_im, zero, c_re], axis=0),
            ],
            axis=1,
        ).astype(BF16)
        rad_copies[i].wait()
        cat = jnp.concatenate([rad[i, p, r] for p in range(2) for r in range(2)], axis=1)
        own[i] = dot(lhs, cat, NT_DIMS).astype(BF16)
        if i == 0:
            pl.semaphore_wait(barrier, 6)
        gathers[0, 0, i].start()
        gathers[1, 0, i].start()

    cur_up = remote(cur_hbm, nbr.at[pl.ds(0, LEAF)], cur_sem.at[0], cur_sem.at[2], dev_up)
    cur_dn = remote(
        cur_hbm, nbr.at[pl.ds(2 * LEAF, LEAF)], cur_sem.at[1], cur_sem.at[3], dev_dn
    )
    cur_up.start()
    cur_dn.start()

    val_copy.wait()
    for b in range(KD // BLK):
        first = ints[O_INTERP + 2 * b]
        second = ints[O_INTERP + 2 * b + 1]
        for q in range(KL // BLK):
            tile = jnp.where(
                first == q,
                val[b, 0],
                jnp.where(second == q, val[b, 1], jnp.zeros((BLK, BLK), BF16)),
            )
            w[pl.ds(b * BLK, BLK), pl.ds(q * BLK, BLK)] = tile
    shift_copy.wait()
    for n in range(NSHIFT):
        row = shift_raw[n].astype(F32)
        for c in range(CH):
            for r in range(2):
                sh[c, n, r] = jnp.broadcast_to(
                    row[r : r + 1, c * KC : (c + 1) * KC], (HALF, KC)
                )

    def lift(rows, first_leaf):
        for c in range(CH):
            moved = dot(rows, w[pl.ds(c * KC, KC), :], NT_DIMS)
            for i in range(LEAF):
                leaf = first_leaf + i
                turn = ints[O_SHIFT + leaf]
                s_re = sh[c, turn, 0]
                s_im = sh[c, turn, 1]
                m_re = moved[i * COMPS : i * COMPS + HALF]
                m_im = moved[i * COMPS + HALF : (i + 1) * COMPS]
                shifted[c, leaf, 0:HALF] = m_re * s_re - m_im * s_im
                shifted[c, leaf, HALF:COMPS] = m_re * s_im + m_im * s_re

    def rows_of(block):
        return block.reshape(LEAF * COMPS, KL)

    def block_of(offset):
        return lax.rem(samp + offset + SAMP, SAMP)

    lift(rows_of(own[...]), block_of(0) * LEAF)

    def near_leaf(i):
        near_copies[i].wait()
        acc = jnp.zeros((HALF, BLK), F32)
        for n in range(NEAR):
            lhs = xbuf[ints[O_NEAR + i * NEAR + n]]
            acc += dot(lhs, jnp.concatenate([near[i, n, 0], near[i, n, 1]], axis=1), NT_DIMS)
        nearacc[i] = acc

    def expand_trans():
        trans_copy.wait()

        def body(n, carry):
            row = trans_raw[n].astype(F32)
            for c in range(CH):
                for r in range(2):
                    tr[c, n, r] = jnp.broadcast_to(
                        row[r : r + 1, c * KC : (c + 1) * KC], (HALF, KC)
                    )
            return carry

        lax.fori_loop(0, NDISP, body, 0)

    for step in range(3):
        for i in range(LEAF):
            for way in range(2):
                gathers[way, step, i].wait_recv()
                if gather_has(way, step + 1, i):
                    gathers[way, step + 1, i].start()
        lift(rows_of(ag_r[step]), block_of(-1 - step) * LEAF)
        lift(rows_of(ag_l[step]), block_of(1 + step) * LEAF)
        if step == 0:
            cur_up.wait_recv()
            cur_dn.wait_recv()
            for m in range(3 * LEAF):
                x = nbr[m].astype(F32)
                turned = jnp.concatenate([-x[EXC:], x[:EXC]], axis=0)
                xbuf[m] = jnp.concatenate([x, turned], axis=1).astype(BF16)
            expand_trans()
        elif step == 1:
            near_leaf(0)
            near_leaf(1)
        else:
            near_leaf(2)
            near_leaf(3)
    for i in range(LEAF):
        way = 0 if i < 2 else 1
        gathers[way, 3, i].wait_recv()
    lift(rows_of(ag_f[...]), block_of(4) * LEAF)

    halos = []
    for c in range(CH):

        def sum_step(j, acc):
            keep = ints[O_CONT + j]
            value = shifted[c, ints[O_ORDER + j]]
            acc = jnp.where(keep == 1, acc, jnp.zeros_like(acc)) + value
            seg[j] = acc
            return acc

        lax.fori_loop(0, GL, sum_step, jnp.zeros((COMPS, KC), F32), unroll=4)

        def top_step(t, carry):
            value = seg[ints[O_LAST + t]]
            value = jnp.where(ints[O_HAS + t] == 1, value, jnp.zeros_like(value)).astype(BF16)
            topbf[c, t] = value
            srcf[c, RIM + t] = value.astype(F32)
            return carry

        lax.fori_loop(0, TOP, top_step, 0, unroll=4)
        up = remote(
            topbf.at[c, pl.ds(TOP - RIM, RIM)],
            halo_l.at[c],
            halo_send.at[0, c],
            halo_recv.at[0, c],
            box_next,
        )
        dn = remote(
            topbf.at[c, pl.ds(0, RIM)],
            halo_r.at[c],
            halo_send.at[1, c],
            halo_recv.at[1, c],
            box_prev,
        )
        up.start()
        dn.start()
        halos.append((up, dn))

    for c in range(CH):
        halos[c][0].wait_recv()
        halos[c][1].wait_recv()

        def widen(t, carry):
            srcf[c, t] = halo_l[c, t].astype(F32)
            srcf[c, RIM + TOP + t] = halo_r[c, t].astype(F32)
            return carry

        lax.fori_loop(0, RIM, widen, 0, unroll=2)

        def move(t, carry):
            acc_re = jnp.zeros((HALF, KC), F32)
            acc_im = jnp.zeros((HALF, KC), F32)
            for j in range(ILIST):
                source = ints[O_SRC + t * ILIST + j]
                disp = ints[O_DISP + t * ILIST + j]
                s_re = srcf[c, source, 0:HALF]
                s_im = srcf[c, source, HALF:COMPS]
                t_re = tr[c, disp, 0]
                t_im = tr[c, disp, 1]
                acc_re += t_re * s_re - t_im * s_im
                acc_im += t_re * s_im + t_im * s_re
            value = jnp.concatenate([acc_re, acc_im], axis=0)
            inc[t] = value.astype(BF16).astype(F32)
            return carry

        lax.fori_loop(0, TOP, move, 0)

        def lower(leaf, carry):
            value = inc[ints[O_PARENT + leaf]]
            turn = ints[O_SHIFT + leaf]
            s_re = sh[c, turn, 0]
            s_im = sh[c, turn, 1]
            v_re, v_im = value[:HALF], value[HALF:]
            d_re = s_re * v_re + s_im * v_im
            d_im = s_re * v_im - s_im * v_re
            down[leaf, :, c * KC : (c + 1) * KC] = jnp.concatenate(
                [d_re, d_im], axis=0
            ).astype(BF16)
            return carry

        lax.fori_loop(0, GL, lower, 0, unroll=4)

    def far_part(offset):
        first = block_of(offset) * LEAF
        rows = down[pl.ds(first, LEAF)].reshape(LEAF * COMPS, KD)
        res = dot(rows, w[...], NN_DIMS).astype(BF16)
        part[pl.ds(first, LEAF)] = res.reshape(LEAF, COMPS, KL)

    def far_src(way, step, i):
        offset = (4 - step) if way == 0 else (step - 4)
        return block_of(offset) * LEAF + i

    def far_first(way, step, i):
        return step == 0 or (step == 1 and (i < 2) == (way == 1))

    def far_has(way, step, i):
        return step > 0 or (i < 2) == (way == 0)

    def far_copy(way, step, i):
        if far_first(way, step, i):
            src = part.at[far_src(way, step, i)]
        else:
            src = (st_r if way == 0 else st_l).at[step, i]
        dst = (rs_r if way == 0 else rs_l).at[step, i]
        return remote(
            src, dst, rs_send.at[way, step, i], rs_recv.at[way, step, i], (right, left)[way]
        )

    fars = {
        (way, step, i): far_copy(way, step, i)
        for step in range(4)
        for i in range(LEAF)
        for way in range(2)
        if far_has(way, step, i)
    }
    orders = ((0, 1, 2, 3), (2, 3, 0, 1))

    far_part(4)
    for k in range(LEAF):
        for way in range(2):
            if far_has(way, 0, orders[way][k]):
                fars[way, 0, orders[way][k]].start()
    for step in range(1, 4):
        far_part(4 - step)
        far_part(step - 4)
        if step == 1:
            for way in range(2):
                for i in range(LEAF):
                    if far_first(way, 1, i):
                        fars[way, 1, i].start()
        if step == 3:
            far_part(0)
        for k in range(LEAF):
            for way in range(2):
                i = orders[way][k]
                if far_first(way, step, i):
                    continue
                fars[way, step - 1, i].wait_recv()
                came = (rs_r if way == 0 else rs_l)[step - 1, i].astype(F32)
                mine = part[far_src(way, step, i)].astype(F32)
                (st_r if way == 0 else st_l)[step, i] = (came + mine).astype(BF16)
                fars[way, step, i].start()

    for i in range(LEAF):
        for way in range(2):
            fars[way, 3, i].wait_recv()
        far = (
            part[samp * LEAF + i].astype(F32)
            + rs_r[3, i].astype(F32)
            + rs_l[3, i].astype(F32)
        ).astype(BF16)
        cat = jnp.concatenate([rad[i, p, r] for p in range(2) for r in range(2)], axis=1)
        g = dot(far, cat, NN_DIMS)
        re = (
            g[0:4, 0:128] + g[8:12, 128:256] + g[4:8, 256:384] + g[12:16, 384:512]
        )
        im = (
            g[8:12, 0:128] - g[0:4, 128:256] + g[12:16, 256:384] - g[4:8, 384:512]
        )
        out_ref[i] = jnp.concatenate([re, im], axis=0) + nearacc[i]

    for copy in gathers.values():
        copy.wait_send()
    cur_up.wait_send()
    cur_dn.wait_send()
    for up, dn in halos:
        up.wait_send()
        dn.wait_send()
    for copy in fars.values():
        copy.wait_send()


def tables(near_src, leaf_parent, leaf_shift, interp_idx, top_src, top_disp):
    group = lax.axis_index("box")
    first_leaf = (group * SAMP + lax.axis_index("samp")) * LEAF
    parent = leaf_parent - group * TOP
    ids = jnp.arange(GL, dtype=jnp.int32)
    key = parent * GL + ids
    rank = jnp.sum((key[None, :] < key[:, None]).astype(jnp.int32), axis=1)
    at = rank[None, :] == ids[:, None]
    order = jnp.sum(jnp.where(at, ids[None, :], 0), axis=1)
    sorted_parent = jnp.sum(jnp.where(at, parent[None, :], 0), axis=1)
    before = jnp.sum(jnp.where(rank[None, :] == ids[:, None] - 1, parent[None, :] + 1, 0), axis=1) - 1
    cont = (before == sorted_parent).astype(jnp.int32)
    boxes = jnp.arange(TOP, dtype=jnp.int32)
    upto = jnp.sum((parent[None, :] <= boxes[:, None]).astype(jnp.int32), axis=1)
    has = jnp.any(parent[None, :] == boxes[:, None], axis=1).astype(jnp.int32)
    last = jnp.maximum(upto - 1, 0)
    return jnp.concatenate(
        [
            order,
            cont,
            last,
            has,
            leaf_shift,
            parent,
            (near_src - first_leaf + LEAF).reshape(-1),
            interp_idx.reshape(-1),
            (top_src - group * TOP + RIM).reshape(-1),
            top_disp.reshape(-1),
        ]
    ).astype(jnp.int32)


def per_device(
    currents,
    radiation,
    near_blocks,
    near_src,
    leaf_parent,
    leaf_shift,
    shift_table,
    interp_idx,
    interp_val,
    top_src,
    top_disp,
    trans_table,
):
    ints = tables(near_src, leaf_parent, leaf_shift, interp_idx, top_src, top_disp)
    boxes = lax.axis_size("box")
    any_spec = pl.BlockSpec(memory_space=pl.ANY)
    dma = pltpu.SemaphoreType.DMA
    vm = pltpu.VMEM
    return pl.pallas_call(
        functools.partial(kernel, boxes),
        out_shape=jax.ShapeDtypeStruct((LEAF, 2 * EXC, 128), F32),
        in_specs=[pl.BlockSpec(memory_space=pltpu.SMEM)] + [any_spec] * 6,
        out_specs=pl.BlockSpec(memory_space=pltpu.VMEM),
        scratch_shapes=[
            vm((3 * LEAF, 8, 128), BF16),
            vm((3 * LEAF, 8, 256), BF16),
            vm((LEAF, 2, 2, KL, 128), BF16),
            vm((LEAF, NEAR, 2, 128, 128), BF16),
            vm((NSHIFT, 2, KD), BF16),
            vm((8, 2, 128, 128), BF16),
            vm((NDISP, 2, KD), BF16),
            vm((KD, KL), BF16),
            vm((CH, NSHIFT, 2, HALF, KC), F32),
            vm((CH, NDISP, 2, HALF, KC), F32),
            vm((LEAF, COMPS, KL), BF16),
            vm((3, LEAF, COMPS, KL), BF16),
            vm((3, LEAF, COMPS, KL), BF16),
            vm((LEAF, COMPS, KL), BF16),
            vm((CH, GL, COMPS, KC), F32),
            vm((GL, COMPS, KC), F32),
            vm((CH, TOP, COMPS, KC), BF16),
            vm((CH, RIM, COMPS, KC), BF16),
            vm((CH, RIM, COMPS, KC), BF16),
            vm((CH, TOP + 2 * RIM, COMPS, KC), F32),
            vm((TOP, COMPS, KC), F32),
            vm((GL, COMPS, KD), BF16),
            vm((GL, COMPS, KL), BF16),
            vm((4, LEAF, COMPS, KL), BF16),
            vm((4, LEAF, COMPS, KL), BF16),
            vm((4, LEAF, COMPS, KL), BF16),
            vm((4, LEAF, COMPS, KL), BF16),
            vm((LEAF, 2 * EXC, 128), F32),
            dma((12,)),
            dma((4,)),
            dma((2, 4, LEAF)),
            dma((2, 4, LEAF)),
            dma((2, CH)),
            dma((2, CH)),
            dma((2, 4, LEAF)),
            dma((2, 4, LEAF)),
        ],
        compiler_params=pltpu.CompilerParams(collective_id=0, has_side_effects=True),
    )(ints, currents, radiation, near_blocks, shift_table, interp_val, trans_table)


def solution(mesh):
    placed = (
        P(("box", "samp"), None, None),
        P(("box", "samp"), None, None, None, None),
        P(("box", "samp"), None, None, None, None),
        P(("box", "samp"), None),
        P("box"),
        P("box"),
        P(None, None, "samp"),
        P("samp", None),
        P("samp", None, None, None),
        P("box", None),
        P("box", None),
        P(None, None, "samp"),
    )
    return jax.shard_map(
        per_device,
        mesh=mesh,
        in_specs=placed,
        out_specs=P(("box", "samp"), None, None),
        check_vma=False,
    )
```

time: 177 us -> 57.8 us (0.33)
  the two profiles are of different devices: /device:TPU:4 before, /device:TPU:64 now
where the time goes in v1:
time: 57.8 us; the launch traced here: 57.3 us
  Pallas kernels  50.2 us (87%)
  local copies, waits for them, and re-layouts  4.43 us (8%)
  other arithmetic  2.7 us (5%)
    pallas_call x1, Pallas kernels, per_device(): pl.pallas_call(functools.partial(kernel, boxes), out_shape=jax.ShapeDtype...  50.2 us
    unnamed x2, local copies, waits for them, and re-layouts  2.08 us
    concatenate x1, local copies, waits for them, and re-layouts, tables(): jnp.concatenate([order, cont, last, has, leaf_shift, parent, (near_src -...  1.32 us

profile of v1, /device:TPU:64, one launch (start us, length us, event | category | flops | bytes accessed | tf_op | source)
XLA Modules:
  0.0 57.3 jit_solution(9734657206751094434)
XLA Ops:
  0.0 0.8 %reshape.26 = s32[256]{0:T(256)S(1)} reshape(s32[16,16]{1,0:T(8,128)} %param.22) | data formatting | bytes 2048 | tf_op jit(solution)/shard_map/reshape | solution.py:483
  0.8 0.7 %subtract_add_fusion.1 = s32[4,8]{1,0:T(4,128)S(1)} fusion(s32[4,8]{1,0:T(4,128)} %param.15, s32[]{:T(128)S(6)} %mul.20), kind=kLoop, calls=%fused_computation.10 | loop fusion | flops 64 | bytes 260 | tf_op jit(solution)/shard_map/add | solution.py:480
  1.5 0.1 reshape.23
  1.5 0.7 %iota_add_fusion.1 = (s32[32]{0:T(128)S(1)}, s32[32]{0:T(128)S(1)}, s32[32]{0:T(128)S(1)}) fusion(s32[32]{0:T(128)} %param.16, s32[]{:T(128)S(6)} %mul.16), kind=kLoop, calls=%fused_computation.14 | loop fusion | flops 128 | bytes 516 | tf_op jit(solution)/shard_map/add | solution.py:461
  2.2 0.2 convert_reduce_fusion
  2.4 0.1 convert_reduce_fusion.1
  2.5 0.2 select_reduce_fusion.1
  2.8 0.1 fusion
  2.9 0.8 %copy.15 = s32[8,2]{1,0:T(8,128)S(1)} copy(s32[8,2]{0,1:T(2,128)} %param.19) | data formatting | bytes 128 | tf_op args[7]
  3.6 0.1 reshape.24
  3.7 0.7 %subtract_add_fusion = s32[16,16]{1,0:T(8,128)S(1)} fusion(s32[16,16]{1,0:T(8,128)} %param.21, s32[]{:T(128)S(6)} %mul.16), kind=kLoop, calls=%fused_computation.5 | loop fusion | flops 512 | bytes 2052 | tf_op jit(solution)/shard_map/add | solution.py:482
  4.4 0.1 reshape.25
  4.5 1.3 %concatenate.3.ints = s32[720]{0:T(1024)} concatenate(s32[32]{0:T(128)S(1)} %get-tuple-element.7, s32[32]{0:T(128)S(1)} %compare_convert_fusion, s32[16]{0:T(128)S(1)} %add_maximum_fusion, s32[16]{0:T(128)S(1)} %convert_element_type.15, s32[32]{0:T(128)} %param.17, s32[32]{0:T(128)S(1)} %get-tuple-element.9, s32[32]{0:T(128)S(1)} %reshape.23, s32[16]{0:T(128)S(1)} %reshape.24, ...), dimensions={0} | concatenate | bytes 5760 | tf_op jit(solution)/shard_map/concatenate | solution.py:472
  5.8 50.2 %shard_map.118 = f32[4,8,128]{2,1,0:T(8,128)} custom-call(s32[720]{0:T(1024)} %concatenate.3.ints, bf16[4,8,128]{2,1,0:T(8,128)(2,1)} %cur_hbm.1, bf16[4,2,2,512,128]{4,3,2,1,0:T(8,128)(2,1)} %rad_hbm.1, bf16[4,8,2,128,128]{4,3,2,1,0:T(8,128)(2,1)} %near_hbm.1, bf16[8,2,1024]{2,1,0:T(2,128)(2,1)} %shift_hbm.1, bf16[8,2,128,128]{3,2,1,0:T(8,128)(2,1)} %val_hbm.1, ...), custom_call_target="tpu_custom_call" | custom-call | tf_op jit(solution)/shard_map/pallas_call | solution.py:507
  56.0 1.3 %copy.17 = f32[4,8,128]{2,1,0:T(8,128)} copy(f32[4,8,128]{2,1,0:T(8,128)} %shard_map.118) | data formatting | bytes 32768
  (4 shorter events, 0.0 us)

commit v2 on v1

v2 whole, which is shorter than its diff:
```python
import functools

import jax
import jax.numpy as jnp
from jax import lax
from jax.experimental import pallas as pl
from jax.experimental.pallas import tpu as pltpu
from jax.sharding import PartitionSpec as P

MESH = pl.DeviceIdType.MESH
F32 = jnp.float32
BF16 = jnp.bfloat16
EXC = 4
COMPS = 16
HALF = 8
KL = 512
KD = 1024
BLK = 128
CH = 4
KC = KD // CH
LEAF = 4
SAMP = 8
GL = LEAF * SAMP
TOP = 16
RIM = 8
NEAR = 8
ILIST = 16
NDISP = 32
NSHIFT = 8

NT_DIMS = (((1,), (1,)), ((), ()))
NN_DIMS = (((1,), (0,)), ((), ()))


def dot(a, b, dims):
    return lax.dot_general(a, b, dims, preferred_element_type=F32)


def kernel(
    boxes,
    parent_hbm,
    turn_hbm,
    near_idx_hbm,
    interp_hbm,
    src_hbm,
    disp_hbm,
    cur_hbm,
    rad_hbm,
    near_hbm,
    shift_hbm,
    val_hbm,
    trans_hbm,
    out_ref,
    parent_s,
    turn_s,
    near_s,
    interp_s,
    src_s,
    disp_s,
    order_s,
    parent_v,
    order_v,
    nbr,
    xbuf,
    rad,
    near,
    shift_raw,
    val,
    trans_raw,
    w,
    sh,
    tr,
    own,
    ag,
    ag_f,
    shifted,
    seg,
    topbf,
    halo_l,
    halo_r,
    srcf,
    inc,
    down,
    part,
    near_in,
    relay_in,
    half_in,
    relay_out,
    end_in,
    nearacc,
    local_sem,
    cur_sem,
    ag_send,
    ag_recv,
    halo_send,
    halo_recv,
    rs_send,
    rs_recv,
):
    box = lax.axis_index("box")
    samp = lax.axis_index("samp")
    total = boxes * SAMP
    ones = [(box, lax.rem(samp + d, SAMP)) for d in (1, SAMP - 1)]
    twos = [(box, lax.rem(samp + d, SAMP)) for d in (2, SAMP - 2)]
    box_next = (lax.rem(box + 1, boxes), samp)
    box_prev = (lax.rem(box + boxes - 1, boxes), samp)
    flat = box * SAMP + samp
    flat_up = lax.rem(flat + 1, total)
    flat_dn = lax.rem(flat + total - 1, total)
    dev_up = (flat_up // SAMP, lax.rem(flat_up, SAMP))
    dev_dn = (flat_dn // SAMP, lax.rem(flat_dn, SAMP))

    def local(src, dst, index):
        return pltpu.make_async_copy(src, dst, local_sem.at[index])

    cur_copy = local(cur_hbm, nbr.at[pl.ds(LEAF, LEAF)], 0)
    rad_copies = [local(rad_hbm.at[i], rad.at[i], 1 + i) for i in range(LEAF)]
    val_copy = local(val_hbm, val, 5)
    shift_copy = local(shift_hbm, shift_raw, 6)
    trans_copy = local(trans_hbm, trans_raw, 7)
    near_copies = [local(near_hbm.at[i], near.at[i], 8 + i) for i in range(LEAF)]
    index_copies = [
        local(src, dst, 12 + k)
        for k, (src, dst) in enumerate(
            (
                (parent_hbm, parent_v),
                (interp_hbm, interp_s),
                (turn_hbm, turn_s),
                (near_idx_hbm, near_s),
                (parent_hbm, parent_s),
                (src_hbm, src_s),
                (disp_hbm, disp_s),
            )
        )
    ]
    order_copy = local(order_v, order_s, 19)
    cur_copy.start()
    for copy in rad_copies:
        copy.start()
    barrier = pltpu.get_barrier_semaphore()
    for dev in (*twos, *ones, box_next, box_prev, dev_up, dev_dn):
        pl.semaphore_signal(barrier, inc=1, device_id=dev, device_id_type=MESH)
    for copy in (val_copy, shift_copy, *index_copies, trans_copy, *near_copies):
        copy.start()

    def remote(src, dst, send, recv, dev):
        return pltpu.make_async_remote_copy(
            src_ref=src,
            dst_ref=dst,
            send_sem=send,
            recv_sem=recv,
            device_id=dev,
            device_id_type=MESH,
        )

    def half(h):
        return pl.ds(2 * h, 2)

    def gather_copy(way, dist, h):
        src = own.at[half(h)] if dist < 3 else ag.at[way, 1, half(h)]
        dst = ag_f.at[half(h)] if dist == 4 else ag.at[way, dist - 1, half(h)]
        dev = (ones if dist % 2 else twos)[way]
        return remote(
            src, dst, ag_send.at[way, dist - 1, h], ag_recv.at[way, dist - 1, h], dev
        )

    gathers = {
        (way, dist, h): gather_copy(way, dist, h)
        for dist in (1, 2, 3, 4)
        for h in range(2)
        for way in range(2)
        if dist < 4 or h == way
    }

    cur_copy.wait()
    for i in range(LEAF):
        x = nbr[LEAF + i].astype(F32)
        c_re, c_im = x[:EXC], x[EXC:]
        zero = jnp.zeros_like(c_re)
        lhs = jnp.concatenate(
            [
                jnp.concatenate([c_re, zero, c_im, zero], axis=0),
                jnp.concatenate([-c_im, zero, c_re, zero], axis=0),
                jnp.concatenate([zero, c_re, zero, c_im], axis=0),
                jnp.concatenate([zero, -c_im, zero, c_re], axis=0),
            ],
            axis=1,
        ).astype(BF16)
        rad_copies[i].wait()
        cat = jnp.concatenate([rad[i, p, r] for p in range(2) for r in range(2)], axis=1)
        own[i] = dot(lhs, cat, NT_DIMS).astype(BF16)
        if i == 1:
            pl.semaphore_wait(barrier, 8)
        if i % 2:
            for dist in (2, 1):
                for way in range(2):
                    gathers[way, dist, i // 2].start()

    cur_up = remote(cur_hbm, nbr.at[pl.ds(0, LEAF)], cur_sem.at[0], cur_sem.at[2], dev_up)
    cur_dn = remote(
        cur_hbm, nbr.at[pl.ds(2 * LEAF, LEAF)], cur_sem.at[1], cur_sem.at[3], dev_dn
    )
    cur_up.start()
    cur_dn.start()

    for copy in index_copies:
        copy.wait()
    order_leaves(parent_v[...] & (TOP - 1), order_v)
    order_copy.start()

    val_copy.wait()
    for b in range(KD // BLK):
        first = interp_s[0, b]
        second = interp_s[1, b]
        for q in range(KL // BLK):
            tile = jnp.where(
                first == q,
                val[b, 0],
                jnp.where(second == q, val[b, 1], jnp.zeros((BLK, BLK), BF16)),
            )
            w[pl.ds(b * BLK, BLK), pl.ds(q * BLK, BLK)] = tile
    shift_copy.wait()
    for n in range(NSHIFT):
        row = shift_raw[n].astype(F32)
        for c in range(CH):
            for r in range(2):
                sh[c, n, r] = jnp.broadcast_to(
                    row[r : r + 1, c * KC : (c + 1) * KC], (HALF, KC)
                )

    def lift(rows, first_leaf):
        for c in range(CH):
            moved = dot(rows, w[pl.ds(c * KC, KC), :], NT_DIMS)
            for i in range(LEAF):
                leaf = first_leaf + i
                turn = turn_s[leaf]
                s_re = sh[c, turn, 0]
                s_im = sh[c, turn, 1]
                m_re = moved[i * COMPS : i * COMPS + HALF]
                m_im = moved[i * COMPS + HALF : (i + 1) * COMPS]
                shifted[c, leaf, 0:HALF] = m_re * s_re - m_im * s_im
                shifted[c, leaf, HALF:COMPS] = m_re * s_im + m_im * s_re

    def rows_of(block):
        return block.reshape(LEAF * COMPS, KL)

    def block_of(offset):
        return lax.rem(samp + offset + SAMP, SAMP)

    lift(rows_of(own[...]), block_of(0) * LEAF)

    def near_leaf(i):
        near_copies[i].wait()
        acc = jnp.zeros((HALF, BLK), F32)
        for n in range(NEAR):
            lhs = xbuf[jnp.clip(near_s[i, n] - (flat - 1) * LEAF, 0, 3 * LEAF - 1)]
            acc += dot(lhs, jnp.concatenate([near[i, n, 0], near[i, n, 1]], axis=1), NT_DIMS)
        nearacc[i] = acc

    def expand_trans():
        trans_copy.wait()

        def body(n, carry):
            row = trans_raw[n].astype(F32)
            for c in range(CH):
                for r in range(2):
                    tr[c, n, r] = jnp.broadcast_to(
                        row[r : r + 1, c * KC : (c + 1) * KC], (HALF, KC)
                    )
            return carry

        lax.fori_loop(0, NDISP, body, 0)

    for h in range(2):
        for way in range(2):
            gathers[way, 2, h].wait_recv()
            if h == way:
                gathers[way, 4, h].start()
            gathers[way, 3, h].start()
    for dist in (2, 1, 3):
        for way in range(2):
            if dist != 2:
                gathers[way, dist, 0].wait_recv()
                gathers[way, dist, 1].wait_recv()
            lift(rows_of(ag[way, dist - 1]), block_of(dist if way else -dist) * LEAF)
    gathers[0, 4, 0].wait_recv()
    gathers[1, 4, 1].wait_recv()
    lift(rows_of(ag_f[...]), block_of(4) * LEAF)

    order_copy.wait()
    halos = []
    for c in range(CH):

        def sum_step(j, acc):
            keep = order_s[1, j]
            value = shifted[c, order_s[0, j]]
            acc = jnp.where(keep == 1, acc, jnp.zeros_like(acc)) + value
            seg[j] = acc
            return acc

        lax.fori_loop(0, GL, sum_step, jnp.zeros((COMPS, KC), F32), unroll=4)

        def top_step(t, carry):
            value = seg[order_s[2, t]]
            value = jnp.where(order_s[3, t] == 1, value, jnp.zeros_like(value)).astype(BF16)
            topbf[c, t] = value
            srcf[c, RIM + t] = value.astype(F32)
            return carry

        lax.fori_loop(0, TOP, top_step, 0, unroll=4)
        up = remote(
            topbf.at[c, pl.ds(TOP - RIM, RIM)],
            halo_l.at[c],
            halo_send.at[0, c],
            halo_recv.at[0, c],
            box_next,
        )
        dn = remote(
            topbf.at[c, pl.ds(0, RIM)],
            halo_r.at[c],
            halo_send.at[1, c],
            halo_recv.at[1, c],
            box_prev,
        )
        up.start()
        dn.start()
        halos.append((up, dn))
    expand_trans()

    for c in range(CH):
        halos[c][0].wait_recv()
        halos[c][1].wait_recv()

        def widen(t, carry):
            srcf[c, t] = halo_l[c, t].astype(F32)
            srcf[c, RIM + TOP + t] = halo_r[c, t].astype(F32)
            return carry

        lax.fori_loop(0, RIM, widen, 0, unroll=2)

        def move(t, carry):
            acc_re = jnp.zeros((HALF, KC), F32)
            acc_im = jnp.zeros((HALF, KC), F32)
            for j in range(ILIST):
                source = (src_s[t, j] - (box * TOP - RIM)) & (2 * TOP - 1)
                disp = disp_s[t, j]
                s_re = srcf[c, source, 0:HALF]
                s_im = srcf[c, source, HALF:COMPS]
                t_re = tr[c, disp, 0]
                t_im = tr[c, disp, 1]
                acc_re += t_re * s_re - t_im * s_im
                acc_im += t_re * s_im + t_im * s_re
            value = jnp.concatenate([acc_re, acc_im], axis=0)
            inc[t] = value.astype(BF16).astype(F32)
            return carry

        lax.fori_loop(0, TOP, move, 0)

        def lower(at, carry):
            leaf = lax.rem(at + samp * LEAF, GL)
            value = inc[parent_s[0, leaf] & (TOP - 1)]
            turn = turn_s[leaf]
            s_re = sh[c, turn, 0]
            s_im = sh[c, turn, 1]
            v_re, v_im = value[:HALF], value[HALF:]
            d_re = s_re * v_re + s_im * v_im
            d_im = s_re * v_im - s_im * v_re
            down[at, :, c * KC : (c + 1) * KC] = jnp.concatenate(
                [d_re, d_im], axis=0
            ).astype(BF16)
            return carry

        lax.fori_loop(0, GL, lower, 0, unroll=8)

    def far_part(first, count):
        rows = down[pl.ds(first * LEAF, count * LEAF)].reshape(count * LEAF * COMPS, KD)
        res = dot(rows, w[...], NN_DIMS).astype(BF16)
        part[pl.ds(first * LEAF, count * LEAF)] = res.reshape(count * LEAF, COMPS, KL)

    def part_half(offset, h):
        return pl.ds((offset % SAMP) * LEAF + 2 * h, 2)

    signs = (1, -1)
    relays = {}
    quarters = {}
    firsts = {}
    seconds = {}
    for way in range(2):
        quarters[way] = remote(
            part.at[part_half(4, way)],
            half_in.at[way],
            rs_send.at[way, 0, 0],
            rs_recv.at[way, 0, 0],
            twos[way],
        )
        firsts[way] = remote(
            part.at[pl.ds((signs[way] % SAMP) * LEAF, LEAF)],
            near_in.at[way],
            rs_send.at[way, 0, 1],
            rs_recv.at[way, 0, 1],
            ones[way],
        )
        for h in range(2):
            relays[way, h] = remote(
                part.at[part_half(3 * signs[way], h)],
                relay_in.at[way, half(h)],
                rs_send.at[way, 1, h],
                rs_recv.at[way, 1, h],
                ones[way],
            )
            seconds[way, h] = remote(
                relay_out.at[way, half(h)],
                end_in.at[way, half(h)],
                rs_send.at[way, 2, h],
                rs_recv.at[way, 2, h],
                twos[way],
            )

    far_part(3, 3)
    for way in range(2):
        quarters[way].start()
        relays[way, 1 - way].start()
    for way in range(2):
        relays[way, way].start()
    far_part(6, 2)
    far_part(1, 2)
    for way in range(2):
        firsts[way].start()
    far_part(0, 1)
    cur_up.wait_recv()
    cur_dn.wait_recv()
    for m in range(3 * LEAF):
        x = nbr[m].astype(F32)
        turned = jnp.concatenate([-x[EXC:], x[:EXC]], axis=0)
        xbuf[m] = jnp.concatenate([x, turned], axis=1).astype(BF16)
    near_leaf(0)
    for way in range(2):
        h = 1 - way
        relays[way, h].wait_recv()
        mine = part[part_half(2 * signs[way], h)].astype(F32)
        relay_out[way, half(h)] = (mine + relay_in[way, half(h)].astype(F32)).astype(BF16)
        seconds[way, h].start()
    for way in range(2):
        h = way
        relays[way, h].wait_recv()
        quarters[way].wait_recv()
        mine = part[part_half(2 * signs[way], h)].astype(F32)
        relay_out[way, half(h)] = (
            mine + relay_in[way, half(h)].astype(F32) + half_in[way].astype(F32)
        ).astype(BF16)
        seconds[way, h].start()
    near_leaf(1)
    near_leaf(2)
    near_leaf(3)
    for way in range(2):
        firsts[way].wait_recv()
    for way in range(2):
        seconds[way, 1 - way].wait_recv()
    for way in range(2):
        seconds[way, way].wait_recv()

    for i in range(LEAF):
        far = (
            part[i].astype(F32)
            + (near_in[0, i].astype(F32) + near_in[1, i].astype(F32))
            + (end_in[0, i].astype(F32) + end_in[1, i].astype(F32))
        ).astype(BF16)
        cat = jnp.concatenate([rad[i, p, r] for p in range(2) for r in range(2)], axis=1)
        g = dot(far, cat, NN_DIMS)
        re = (
            g[0:4, 0:128] + g[8:12, 128:256] + g[4:8, 256:384] + g[12:16, 384:512]
        )
        im = (
            g[8:12, 0:128] - g[0:4, 128:256] + g[12:16, 256:384] - g[4:8, 384:512]
        )
        out_ref[i] = jnp.concatenate([re, im], axis=0) + nearacc[i]

    for copy in gathers.values():
        copy.wait_send()
    cur_up.wait_send()
    cur_dn.wait_send()
    for up, dn in halos:
        up.wait_send()
        dn.wait_send()
    for group in (quarters, firsts, relays, seconds):
        for copy in group.values():
            copy.wait_send()


def order_leaves(row, table):
    wide = (GL, GL)
    ups = lax.broadcasted_iota(jnp.int32, wide, 0)
    ids = lax.broadcasted_iota(jnp.int32, wide, 1)
    row = jnp.broadcast_to(row, wide)
    col = jnp.sum(jnp.where(ups == ids, row, 0), axis=1, keepdims=True)
    col = jnp.broadcast_to(col, wide)
    lower = (row * GL + ids) < (col * GL + ups)
    rank = jnp.sum(lower.astype(jnp.int32), axis=1, keepdims=True)
    rank = jnp.broadcast_to(rank, wide)
    at = rank == ids

    def total(value):
        return jnp.sum(value, axis=0, keepdims=True)

    order = total(jnp.where(at, ups, 0))
    here = total(jnp.where(at, col, 0))
    before = total(jnp.where(rank == ids - 1, col + 1, 0)) - 1
    last = jnp.maximum(total((col <= ids).astype(jnp.int32)) - 1, 0)
    has = jnp.minimum(total((col == ids).astype(jnp.int32)), 1)
    table[...] = jnp.zeros_like(table)
    table[0:1, 0:GL] = order
    table[1:2, 0:GL] = (before == here).astype(jnp.int32)
    table[2:3, 0:GL] = last
    table[3:4, 0:GL] = has


def per_device(
    currents,
    radiation,
    near_blocks,
    near_src,
    leaf_parent,
    leaf_shift,
    shift_table,
    interp_idx,
    interp_val,
    top_src,
    top_disp,
    trans_table,
):
    boxes = lax.axis_size("box")
    any_spec = pl.BlockSpec(memory_space=pl.ANY)
    dma = pltpu.SemaphoreType.DMA
    vm = pltpu.VMEM
    sm = pltpu.SMEM
    i32 = jnp.int32
    return pl.pallas_call(
        functools.partial(kernel, boxes),
        out_shape=jax.ShapeDtypeStruct((LEAF, 2 * EXC, 128), F32),
        in_specs=[any_spec] * 12,
        out_specs=pl.BlockSpec(memory_space=pltpu.VMEM),
        scratch_shapes=[
            sm((1, GL), i32),
            sm((GL,), i32),
            sm((LEAF, NEAR), i32),
            sm((2, 8), i32),
            sm((TOP, ILIST), i32),
            sm((TOP, ILIST), i32),
            sm((8, 128), i32),
            vm((1, GL), i32),
            vm((8, 128), i32),
            vm((3 * LEAF, 8, 128), BF16),
            vm((3 * LEAF, 8, 256), BF16),
            vm((LEAF, 2, 2, KL, 128), BF16),
            vm((LEAF, NEAR, 2, 128, 128), BF16),
            vm((NSHIFT, 2, KD), BF16),
            vm((8, 2, 128, 128), BF16),
            vm((NDISP, 2, KD), BF16),
            vm((KD, KL), BF16),
            vm((CH, NSHIFT, 2, HALF, KC), F32),
            vm((CH, NDISP, 2, HALF, KC), F32),
            vm((LEAF, COMPS, KL), BF16),
            vm((2, 3, LEAF, COMPS, KL), BF16),
            vm((LEAF, COMPS, KL), BF16),
            vm((CH, GL, COMPS, KC), F32),
            vm((GL, COMPS, KC), F32),
            vm((CH, TOP, COMPS, KC), BF16),
            vm((CH, RIM, COMPS, KC), BF16),
            vm((CH, RIM, COMPS, KC), BF16),
            vm((CH, TOP + 2 * RIM, COMPS, KC), F32),
            vm((TOP, COMPS, KC), F32),
            vm((GL, COMPS, KD), BF16),
            vm((GL, COMPS, KL), BF16),
            vm((2, LEAF, COMPS, KL), BF16),
            vm((2, LEAF, COMPS, KL), BF16),
            vm((2, 2, COMPS, KL), BF16),
            vm((2, LEAF, COMPS, KL), BF16),
            vm((2, LEAF, COMPS, KL), BF16),
            vm((LEAF, 2 * EXC, 128), F32),
            dma((20,)),
            dma((4,)),
            dma((2, 4, 2)),
            dma((2, 4, 2)),
            dma((2, CH)),
            dma((2, CH)),
            dma((2, 3, 2)),
            dma((2, 3, 2)),
        ],
        compiler_params=pltpu.CompilerParams(collective_id=0, has_side_effects=True),
    )(leaf_parent.reshape(1, GL), leaf_shift, near_src, interp_idx.T, top_src, top_disp, currents, radiation, near_blocks, shift_table, interp_val, trans_table)


def solution(mesh):
    placed = (
        P(("box", "samp"), None, None),
        P(("box", "samp"), None, None, None, None),
        P(("box", "samp"), None, None, None, None),
        P(("box", "samp"), None),
        P("box"),
        P("box"),
        P(None, None, "samp"),
        P("samp", None),
        P("samp", None, None, None),
        P("box", None),
        P("box", None),
        P(None, None, "samp"),
    )
    return jax.shard_map(
        per_device,
        mesh=mesh,
        in_specs=placed,
        out_specs=P(("box", "samp"), None, None),
        check_vma=False,
    )
```

time: 57.8 us -> 43.1 us (0.75)
  Pallas kernels: 50.2 us -> 41.5 us
  local copies, waits for them, and re-layouts: 4.43 us -> 1.32 us
  other arithmetic: 2.7 us -> 0 us
    pallas_call x1, Pallas kernels: 50.2 us -> 41.5 us  [per_device(): pl.pallas_call(functools.partial(kernel, boxes), out_shape=jax.ShapeDtype...]
    add x4 -> x0, other arithmetic: 2.06 us -> none  [the longest x1 0.7 us: tables(): top_src - group * TOP + RIM]
    concatenate x1 -> x0, local copies, waits for them, and re-layouts: 1.32 us -> none  [tables(): jnp.concatenate([order, cont, last, has, leaf_shift, parent, (near_src -...]
    reshape x4 -> x0, local copies, waits for them, and re-layouts: 1.02 us -> none  [the longest x1 0.77 us: tables(): top_disp.reshape(-1)]
    unnamed x2 -> x1, local copies, waits for them, and re-layouts: 2.08 us -> 1.32 us
where the time goes in v2:
time: 43.1 us; the launch traced here: 42.8 us
  Pallas kernels  41.5 us (96%)
  local copies, waits for them, and re-layouts  1.32 us (3%)
    pallas_call x1, Pallas kernels, per_device(): pl.pallas_call(functools.partial(kernel, boxes), out_shape=jax.ShapeDtype...  41.5 us
    unnamed x1, local copies, waits for them, and re-layouts  1.32 us

profile of v2, /device:TPU:64, one launch (start us, length us, event | category | flops | bytes accessed | tf_op | source)
XLA Modules:
  0.0 42.8 jit_solution(5529700805117791954)
XLA Ops:
  0.0 41.5 %shard_map.118 = f32[4,8,128]{2,1,0:T(8,128)} custom-call(s32[1,32]{1,0:T(1,128)} %bitcast.3, s32[32]{0:T(128)} %turn_hbm.1, s32[4,8]{1,0:T(4,128)} %near_idx_hbm.1, s32[2,8]{1,0:T(2,128)} %bitcast.2, s32[16,16]{1,0:T(8,128)} %src_hbm.1, s32[16,16]{1,0:T(8,128)} %disp_hbm.1, bf16[4,8,128]{2,1,0:T(8,128)(2,1)} %cur_hbm.1, ...), custom_call_target="tpu_custom_call" | custom-call | tf_op jit(solution)/shard_map/pallas_call | solution.py:537
  41.5 1.3 %copy.14 = f32[4,8,128]{2,1,0:T(8,128)} copy(f32[4,8,128]{2,1,0:T(8,128)} %shard_map.118) | data formatting | bytes 32768

commit v3 on v2

--- a/solution.py
+++ b/solution.py
@@ -192,9 +192,11 @@
         if i == 1:
             pl.semaphore_wait(barrier, 8)
         if i % 2:
-            for dist in (2, 1):
-                for way in range(2):
-                    gathers[way, dist, i // 2].start()
+            for way in range(2):
+                gathers[way, 2, i // 2].start()
+    for h in range(2):
+        for way in range(2):
+            gathers[way, 1, h].start()
 
     cur_up = remote(cur_hbm, nbr.at[pl.ds(0, LEAF)], cur_sem.at[0], cur_sem.at[2], dev_up)
     cur_dn = remote(
@@ -228,8 +230,8 @@
                     row[r : r + 1, c * KC : (c + 1) * KC], (HALF, KC)
                 )
 
-    def lift(rows, first_leaf):
-        for c in range(CH):
+    def lift(rows, first_leaf, chunks=range(CH)):
+        for c in chunks:
             moved = dot(rows, w[pl.ds(c * KC, KC), :], NT_DIMS)
             for i in range(LEAF):
                 leaf = first_leaf + i
@@ -285,11 +287,10 @@
             lift(rows_of(ag[way, dist - 1]), block_of(dist if way else -dist) * LEAF)
     gathers[0, 4, 0].wait_recv()
     gathers[1, 4, 1].wait_recv()
-    lift(rows_of(ag_f[...]), block_of(4) * LEAF)
-
     order_copy.wait()
     halos = []
     for c in range(CH):
+        lift(rows_of(ag_f[...]), block_of(4) * LEAF, (c,))
 
         def sum_step(j, acc):
             keep = order_s[1, j]
@@ -298,7 +299,7 @@
             seg[j] = acc
             return acc
 
-        lax.fori_loop(0, GL, sum_step, jnp.zeros((COMPS, KC), F32), unroll=4)
+        lax.fori_loop(0, GL, sum_step, jnp.zeros((COMPS, KC), F32), unroll=16)
 
         def top_step(t, carry):
             value = seg[order_s[2, t]]
@@ -307,7 +308,7 @@
             srcf[c, RIM + t] = value.astype(F32)
             return carry
 
-        lax.fori_loop(0, TOP, top_step, 0, unroll=4)
+        lax.fori_loop(0, TOP, top_step, 0, unroll=16)
         up = remote(
             topbf.at[c, pl.ds(TOP - RIM, RIM)],
             halo_l.at[c],
@@ -354,7 +355,7 @@
             inc[t] = value.astype(BF16).astype(F32)
             return carry
 
-        lax.fori_loop(0, TOP, move, 0)
+        lax.fori_loop(0, TOP, move, 0, unroll=2)
 
         def lower(at, carry):
             leaf = lax.rem(at + samp * LEAF, GL)
@@ -370,7 +371,7 @@
             ).astype(BF16)
             return carry
 
-        lax.fori_loop(0, GL, lower, 0, unroll=8)
+        lax.fori_loop(0, GL, lower, 0, unroll=16)
 
     def far_part(first, count):
         rows = down[pl.ds(first * LEAF, count * LEAF)].reshape(count * LEAF * COMPS, KD)
@@ -536,7 +537,7 @@
     i32 = jnp.int32
     return pl.pallas_call(
         functools.partial(kernel, boxes),
-        out_shape=jax.ShapeDtypeStruct((LEAF, 2 * EXC, 128), F32),
+        out_shape=pltpu.VMEM((LEAF, 2 * EXC, 128), F32),
         in_specs=[any_spec] * 12,
         out_specs=pl.BlockSpec(memory_space=pltpu.VMEM),
         scratch_shapes=[

time: 43.1 us -> 40.8 us (0.947)
  Pallas kernels: 41.5 us -> 40 us
  local copies, waits for them, and re-layouts: 1.32 us -> 0.61 us
    pallas_call x1, Pallas kernels: 41.5 us -> 40 us  [per_device(): pl.pallas_call(functools.partial(kernel, boxes), out_shape=pltpu.VMEM((LE...]
    unnamed x1, local copies, waits for them, and re-layouts: 1.32 us -> 0.61 us
where the time goes in v3:
time: 40.8 us; the launch traced here: 40.6 us
  Pallas kernels  40 us (98%)
  local copies, waits for them, and re-layouts  0.61 us (1%)
    pallas_call x1, Pallas kernels, per_device(): pl.pallas_call(functools.partial(kernel, boxes), out_shape=pltpu.VMEM((LE...  40 us

profile of v3, /device:TPU:64, one launch (start us, length us, event | category | flops | bytes accessed | tf_op | source)
XLA Modules:
  0.0 40.6 jit_solution(5431117104976675567)
XLA Ops:
  0.0 40.0 %shard_map.118 = f32[4,8,128]{2,1,0:T(8,128)S(1)} custom-call(s32[1,32]{1,0:T(1,128)} %bitcast.3, s32[32]{0:T(128)} %turn_hbm.1, s32[4,8]{1,0:T(4,128)} %near_idx_hbm.1, s32[2,8]{1,0:T(2,128)} %bitcast.2, s32[16,16]{1,0:T(8,128)} %src_hbm.1, s32[16,16]{1,0:T(8,128)} %disp_hbm.1, bf16[4,8,128]{2,1,0:T(8,128)(2,1)} %cur_hbm.1, ...), custom_call_target="tpu_custom_call" | custom-call | tf_op jit(solution)/shard_map/pallas_call | solution.py:538
  40.0 0.6 %copy.14 = f32[4,8,128]{2,1,0:T(8,128)} copy(f32[4,8,128]{2,1,0:T(8,128)S(1)} %shard_map.118) | data formatting | bytes 32768

commit v4 on v3

--- a/solution.py
+++ b/solution.py
@@ -169,8 +169,12 @@
         for dist in (1, 2, 3, 4)
         for h in range(2)
         for way in range(2)
-        if dist < 4 or h == way
+        if dist in (2, 3) or (dist == 4 and h == way)
     }
+    for way in range(2):
+        gathers[way, 1, 0] = remote(
+            own, ag.at[way, 0], ag_send.at[way, 0, 0], ag_recv.at[way, 0, 0], ones[way]
+        )
 
     cur_copy.wait()
     for i in range(LEAF):
@@ -194,9 +198,8 @@
         if i % 2:
             for way in range(2):
                 gathers[way, 2, i // 2].start()
-    for h in range(2):
-        for way in range(2):
-            gathers[way, 1, h].start()
+    for way in range(2):
+        gathers[way, 1, 0].start()
 
     cur_up = remote(cur_hbm, nbr.at[pl.ds(0, LEAF)], cur_sem.at[0], cur_sem.at[2], dev_up)
     cur_dn = remote(
@@ -283,7 +286,8 @@
         for way in range(2):
             if dist != 2:
                 gathers[way, dist, 0].wait_recv()
-                gathers[way, dist, 1].wait_recv()
+                if dist > 1:
+                    gathers[way, dist, 1].wait_recv()
             lift(rows_of(ag[way, dist - 1]), block_of(dist if way else -dist) * LEAF)
     gathers[0, 4, 0].wait_recv()
     gathers[1, 4, 1].wait_recv()
@@ -424,9 +428,24 @@
     for way in range(2):
         relays[way, way].start()
     far_part(6, 2)
+    firsts[1].start()
     far_part(1, 2)
-    for way in range(2):
-        firsts[way].start()
+    firsts[0].start()
+    for way in range(2):
+        h = 1 - way
+        relays[way, h].wait_recv()
+        mine = part[part_half(2 * signs[way], h)].astype(F32)
+        relay_out[way, half(h)] = (mine + relay_in[way, half(h)].astype(F32)).astype(BF16)
+        seconds[way, h].start()
+    for way in range(2):
+        h = way
+        relays[way, h].wait_recv()
+        quarters[way].wait_recv()
+        mine = part[part_half(2 * signs[way], h)].astype(F32)
+        relay_out[way, half(h)] = (
+            mine + relay_in[way, half(h)].astype(F32) + half_in[way].astype(F32)
+        ).astype(BF16)
+        seconds[way, h].start()
     far_part(0, 1)
     cur_up.wait_recv()
     cur_dn.wait_recv()
@@ -435,21 +454,6 @@
         turned = jnp.concatenate([-x[EXC:], x[:EXC]], axis=0)
         xbuf[m] = jnp.concatenate([x, turned], axis=1).astype(BF16)
     near_leaf(0)
-    for way in range(2):
-        h = 1 - way
-        relays[way, h].wait_recv()
-        mine = part[part_half(2 * signs[way], h)].astype(F32)
-        relay_out[way, half(h)] = (mine + relay_in[way, half(h)].astype(F32)).astype(BF16)
-        seconds[way, h].start()
-    for way in range(2):
-        h = way
-        relays[way, h].wait_recv()
-        quarters[way].wait_recv()
-        mine = part[part_half(2 * signs[way], h)].astype(F32)
-        relay_out[way, half(h)] = (
-            mine + relay_in[way, half(h)].astype(F32) + half_in[way].astype(F32)
-        ).astype(BF16)
-        seconds[way, h].start()
     near_leaf(1)
     near_leaf(2)
     near_leaf(3)

time: 40.8 us -> 40.8 us (level)
  no operation moved by 1% of the time
where the time goes in v4:
time: 40.8 us; the launch traced here: 40.6 us
  Pallas kernels  40 us (98%)
  local copies, waits for them, and re-layouts  0.61 us (1%)
    pallas_call x1, Pallas kernels, per_device(): pl.pallas_call(functools.partial(kernel, boxes), out_shape=pltpu.VMEM((LE...  40 us

profile of v4, /device:TPU:64, one launch (start us, length us, event | category | flops | bytes accessed | tf_op | source)
XLA Modules:
  0.0 40.6 jit_solution(7792890853281885649)
XLA Ops:
  0.0 40.0 %shard_map.118 = f32[4,8,128]{2,1,0:T(8,128)S(1)} custom-call(s32[1,32]{1,0:T(1,128)} %bitcast.3, s32[32]{0:T(128)} %turn_hbm.1, s32[4,8]{1,0:T(4,128)} %near_idx_hbm.1, s32[2,8]{1,0:T(2,128)} %bitcast.2, s32[16,16]{1,0:T(8,128)} %src_hbm.1, s32[16,16]{1,0:T(8,128)} %disp_hbm.1, bf16[4,8,128]{2,1,0:T(8,128)(2,1)} %cur_hbm.1, ...), custom_call_target="tpu_custom_call" | custom-call | tf_op jit(solution)/shard_map/pallas_call | solution.py:542
  40.0 0.6 %copy.14 = f32[4,8,128]{2,1,0:T(8,128)} copy(f32[4,8,128]{2,1,0:T(8,128)S(1)} %shard_map.118) | data formatting | bytes 32768
